TPU v7x, 128 devices: a whole 4x4x4 slice. The times are simulated.
128 devices in a mesh: head: 8 (over z, core), query: 8 (over x, y_lo), ctx: 2 (over y_hi).
Axes of the slice: x: 4, y: 4 (y_hi: 2, y_lo: 2; y = y_hi * 2 + y_lo), z: 4, core: 2. Of those that a mesh axis runs over, the one named last changes fastest.
Arguments:
- queries: bfloat16 [1024, 128, 576], P('query', 'head'), may hold values from -3 to 3, as said below
- latent: bfloat16 [4096, 576], P(('head', 'query', 'ctx')), may hold values from -8 to 8
- out_grad: bfloat16 [1024, 128, 512], P('query', 'head'), may hold values from -6 to 6
- log_norms: float32 [1024, 128], P('query', 'head'), as said below
- row_dots: float32 [1024, 128], P('query', 'head'), may hold values from -48 to 48
Outputs:
- query_grad: float32 [1024, 128, 576], P(('query', 'ctx'), 'head')
- latent_grad: float32 [4096, 576], P(('head', 'query', 'ctx'))
Inputs may be any that keep to these rules, and one draw needn't show every extreme that they name: queries and latent are of order one; latent rows may differ in scale. log_norms[i,h] is the log of the sum over all 4096 latent rows of exp(scores[i,h,j]), computed from the given queries and latent.
All inputs are finite; a program needn't handle non-finite values.
Results may differ from a plain program's by a relative error of at most 0.0029.
Values may be sent and summed in bfloat16 or wider, within the bound.
No kernel may reach another device: no remote copies, remote signals or barrier semaphores. Data moves between devices by JAX's collectives and lax.ppermute only.
A program may use at most 64 MiB of HBM per device.

v0:
```python
import math
import jax
import jax.numpy as jnp
from jax import lax
from jax.sharding import PartitionSpec as P

softmax_scale = 192.0 ** (-0.5) * (0.1 * math.log(40.0) + 1.0) ** 2


def tile_grads(flat_q, flat_dout, norms, dots, latent_block):
    value_width = flat_dout.shape[1]
    key_width = latent_block.shape[1]
    scores = (
        lax.dot_general(
            flat_q, latent_block, (((1,), (1,)), ((), ())), preferred_element_type=jnp.float32
        )
        * softmax_scale
    )
    probs = jnp.exp(scores - norms[:, None])
    probs_low = probs.astype(jnp.bfloat16)
    dprobs = lax.dot_general(
        flat_dout,
        latent_block[:, :value_width],
        (((1,), (1,)), ((), ())),
        preferred_element_type=jnp.float32,
    )
    dscores = (probs * (dprobs - dots[:, None])).astype(jnp.bfloat16)
    query_part = jnp.dot(dscores, latent_block, preferred_element_type=jnp.float32)
    latent_key = (
        lax.dot_general(
            dscores, flat_q, (((0,), (0,)), ((), ())), preferred_element_type=jnp.float32
        )
        * softmax_scale
    )
    latent_value = lax.dot_general(
        probs_low, flat_dout, (((0,), (0,)), ((), ())), preferred_element_type=jnp.float32
    )
    latent_part = latent_key + jnp.pad(latent_value, ((0, 0), (0, key_width - value_width)))
    return (query_part, latent_part)


def span_grads(flat_q, flat_dout, norms, dots, latent_rows):
    row_count = latent_rows.shape[0]
    key_width = latent_rows.shape[1]
    block_rows = 512
    stacked = latent_rows.reshape(row_count // block_rows, block_rows, key_width)

    def single(carry, latent_block):
        query_part, latent_part = tile_grads(flat_q, flat_dout, norms, dots, latent_block)
        return (carry + query_part, latent_part)

    initial = jnp.zeros((flat_q.shape[0], key_width), jnp.float32)
    query_sum, latent_parts = lax.scan(single, initial, stacked)
    return (query_sum, latent_parts.reshape(row_count, key_width))


def on_device(queries, latent, out_grad, log_norms, row_dots):
    local_queries, local_heads, key_width = queries.shape
    flat_rows = local_queries * local_heads
    flat_q = queries.reshape(flat_rows, key_width)
    flat_dout = out_grad.reshape(flat_rows, out_grad.shape[2])
    norms = log_norms.reshape(flat_rows)
    dots = row_dots.reshape(flat_rows)
    gathered = lax.all_gather(latent, ("head", "query"), axis=0, tiled=True)
    query_sum, latent_all = span_grads(flat_q, flat_dout, norms, dots, gathered)
    latent_grad = lax.psum_scatter(latent_all, ("head", "query"), scatter_dimension=0, tiled=True)
    query_terms = (query_sum * softmax_scale).reshape(local_queries, local_heads, key_width)
    query_grad = lax.psum_scatter(query_terms, "ctx", scatter_dimension=0, tiled=True)
    return (query_grad, latent_grad)


def solution(mesh):
    in_specs = (
        P("query", "head", None),
        P(("head", "query", "ctx"), None),
        P("query", "head", None),
        P("query", "head"),
        P("query", "head"),
    )
    out_specs = (P(("query", "ctx"), "head", None), P(("head", "query", "ctx"), None))
    return jax.shard_map(
        on_device, mesh=mesh, in_specs=in_specs, out_specs=out_specs, check_vma=False
    )
```

profile of v0, /device:TPU:1, one launch (start us, length us, event | category | flops | bytes accessed | tf_op | source)
XLA Modules:
  0.0 596.4 jit_solution(4269715359291730156)
XLA Ops:
  7.2 0.0 all-gather.2.cloned.1.call-start
  7.2 0.7 all-gather.2.cloned.1.call-update
  7.9 0.0 reduce-scatter.5.cloned.1.call-start
  8.0 0.8 copy.11
  8.8 0.1 sub.60
  8.8 0.8 copy.12
  9.7 0.1 sub.59
  9.7 3.9 copy.10
  13.7 157.6 %all-gather.2.cloned.1.call-done = bf16[2048,576]{1,0:T(8,128)(2,1)} async-done(((bf16[32,576]{1,0:T(8,128)(2,1)}), bf16[2048,576]{1,0:T(8,128)(2,1)}) %all-gather.2.cloned.1.call-update) | async-done | bytes 2359312 | tf_op jit(solution)/shard_map/all_gather | solution.py:64
  171.3 49.7 %while.16 = (s32[]{:T(128)}, f32[2048,576]{0,1:T(8,128)}, f32[4,512,576]{1,2,0:T(8,128)}, bf16[4,512,576]{2,1,0:T(8,128)(2,1)}, bf16[2048,576]{1,0:T(8,128)(2,1)...) while((s32[]{:T(128)}, f32[2048,576]{0,1:T(8,128)}, ...), condition=%wide.wide.region_1.2_spmd.clone, body=%wide.wide.region_0.1_spmd.clone.sunk | while | flops 5782700032 | bytes 84828408 | solution.py:53
  171.3 1.1 dynamic-slice_bitcast_fusion.3
  172.4 0.0 copy-start.3
  172.4 1.8 fusion.55
  174.3 1.3 fusion.56
  175.6 1.3 multiply_convert_fusion.3
  177.0 2.4 fusion.57
  179.4 2.1 select_add_fusion.3
  181.6 2.1 copy-done
  183.7 1.1 dynamic-slice_bitcast_fusion.3
  184.8 0.0 copy-start.3
  184.9 1.8 fusion.55
  186.7 1.3 fusion.56
  188.0 1.3 multiply_convert_fusion.3
  189.4 2.4 fusion.57
  191.8 2.1 select_add_fusion.3
  194.0 2.1 copy-done
  196.1 1.1 dynamic-slice_bitcast_fusion.3
  197.3 1.8 fusion.55
  199.1 1.3 fusion.56
  200.4 1.3 multiply_convert_fusion.3
  201.8 2.5 fusion.57
  204.3 2.1 select_add_fusion.3
  206.4 2.1 copy-done
  208.6 1.1 dynamic-slice_bitcast_fusion.3
  209.7 1.8 fusion.55
  211.6 1.3 fusion.56
  212.9 1.3 multiply_convert_fusion.3
  214.3 2.4 fusion.57
  216.7 2.1 select_add_fusion.3
  218.8 2.1 copy-done
  221.0 5.8 copy.14
  226.7 0.0 reduce-scatter.5.cloned.1.call-update
  226.8 0.0 reduce-scatter.3.cloned.1.call-start
  226.8 5.4 broadcast_multiply_fusion
  232.3 5.8 copy.13
  238.1 0.0 reduce-scatter.3.cloned.1.call-update
  238.1 272.0 %reduce-scatter.5.cloned.1.call-done = f32[32,576]{1,0:T(8,128)} async-done(((f32[2048,576]{1,0:T(8,128)}), f32[32,576]{1,0:T(8,128)}) %reduce-scatter.5.cloned.1.call-update) | async-done | bytes 73744 | tf_op jit(solution)/shard_map/reduce_scatter | solution.py:66
  510.1 79.8 %reduce-scatter.3.cloned.1.call-done = f32[64,16,576]{2,1,0:T(8,128)} async-done(((f32[128,16,576]{2,1,0:T(8,128)}), f32[64,16,576]{2,1,0:T(8,128)}) %reduce-scatter.3.cloned.1.call-update) | async-done | bytes 2359312 | tf_op jit(solution)/shard_map/reduce_scatter | solution.py:68
  (36 shorter events, 0.1 us)
Async XLA Ops:
  7.2 164.1 %all-gather.2.cloned.1.call-start = ((), (), s32[]{:S(2)}) async-start(), calls=%async_computation.2 | async-start | bytes 2662400 | tf_op jit(solution)/shard_map/all_gather | solution.py:64
  7.9 502.2 %reduce-scatter.5.cloned.1.call-start = ((), (), s32[]{:S(2)}) async-start(), calls=%async_computation.4 | async-start | bytes 5324800 | tf_op jit(solution)/shard_map/reduce_scatter | solution.py:66
  8.8 162.5 %copy-start.1 = (f32[128,16]{1,0:T(8,128)}, f32[128,16]{1,0:T(8,128)S(1)}, u32[]{:S(2)}) copy-start(f32[128,16]{1,0:T(8,128)S(1)} %copy.11) | copy-start | bytes 24580
  9.6 161.6 %copy-start.2 = (f32[128,16]{1,0:T(8,128)}, f32[128,16]{1,0:T(8,128)S(1)}, u32[]{:S(2)}) copy-start(f32[128,16]{1,0:T(8,128)S(1)} %copy.12) | copy-start | bytes 24580
  172.4 1.8 copy-start.3
  175.6 3.8 slice-start
  177.0 2.5 slice-start.1
  181.6 2.1 copy-start
  184.8 1.8 copy-start.3
  188.0 3.8 slice-start
  189.4 2.5 slice-start.1
  194.0 2.1 copy-start
  197.3 1.8 copy-start.3
  200.4 3.9 slice-start
  201.8 2.5 slice-start.1
  206.4 2.1 copy-start
  209.7 1.8 copy-start.3
  212.9 3.8 slice-start
  214.3 2.5 slice-start.1
  218.8 2.1 copy-start
  226.8 363.1 %reduce-scatter.3.cloned.1.call-start = ((), (), s32[]{:S(2)}) async-start(), calls=%async_computation.3 | async-start | bytes 7864320 | tf_op jit(solution)/shard_map/reduce_scatter | solution.py:68
Sparse Core Ops, SparseCore 0:
  9.7 161.5 all-gather.1
  226.9 283.1 reduce-scatter.4
  513.1 76.7 reduce-scatter.2
where the time goes:
time: 597 us; the launch traced here: 596 us
  waiting for transfers between devices  510 us (85%)
  matrix products  36.2 us (6%)
  local copies, waits for them, and re-layouts  30.5 us (5%)
  between operations  13.8 us (2%)
    reduce_scatter x1, waiting for transfers between devices, on_device(): lax.psum_scatter(latent_all, ('head', 'query'), scatter_dimension=0, tile...  272 us
    all_gather x1, waiting for transfers between devices, on_device(): gathered = lax.all_gather(latent, ('head', 'query'), axis=0, tiled=True)  158 us
    reduce_scatter x1, waiting for transfers between devices, on_device(): lax.psum_scatter(query_terms, 'ctx', scatter_dimension=0, tiled=True)  79.8 us
  transfers between devices with their start and end apart: 3, of which 3 were waited for; matrix products, arithmetic and copies ran while one was open for 3% of the time, Pallas kernels for 0%

commit v1 on v0

--- a/solution.py
+++ b/solution.py
@@ -61,7 +61,12 @@
     flat_dout = out_grad.reshape(flat_rows, out_grad.shape[2])
     norms = log_norms.reshape(flat_rows)
     dots = row_dots.reshape(flat_rows)
-    gathered = lax.all_gather(latent, ("head", "query"), axis=0, tiled=True)
+    gathered = jnp.concatenate(
+        lax.all_to_all(
+            jnp.stack([latent] * lax.axis_size(("head", "query"))), ("head", "query"), 0, 0
+        ),
+        axis=0,
+    )
     query_sum, latent_all = span_grads(flat_q, flat_dout, norms, dots, gathered)
     latent_grad = lax.psum_scatter(latent_all, ("head", "query"), scatter_dimension=0, tiled=True)
     query_terms = (query_sum * softmax_scale).reshape(local_queries, local_heads, key_width)

time: 597 us -> 485 us (0.81)
  waiting for transfers between devices: 510 us -> 380 us
  starting transfers between devices: 0.12 us -> 10.9 us
  matrix products: 36.2 us -> 43.8 us
    all_gather x1 -> x0, waiting for transfers between devices: 158 us -> none  [on_device(): gathered = lax.all_gather(latent, ('head', 'query'), axis=0, tiled=True)]
    all_to_all x0 -> x1, waiting for transfers between devices: none -> 29.2 us  [on_device(): lax.all_to_all(jnp.stack([latent] * lax.axis_size(('head', 'query'))), ('...]
    all_to_all x0 -> x1, starting transfers between devices: none -> 10.8 us  [on_device(): lax.all_to_all(jnp.stack([latent] * lax.axis_size(('head', 'query'))), ('...]
    dot_general x4, matrix products: 7.3 us -> 14.9 us  [tile_grads(): lax.dot_general(flat_q, latent_block, (((1,), (1,)), ((), ())), preferred...]
where the time goes in v1:
time: 485 us; the launch traced here: 484 us
  waiting for transfers between devices  380 us (78%)
  matrix products  43.8 us (9%)
  local copies, waits for them, and re-layouts  29.8 us (6%)
  between operations  14.1 us (3%)
  starting transfers between devices  10.9 us (2%)
  other arithmetic  5.44 us (1%)
    reduce_scatter x1, waiting for transfers between devices, on_device(): lax.psum_scatter(latent_all, ('head', 'query'), scatter_dimension=0, tile...  271 us
    reduce_scatter x1, waiting for transfers between devices, on_device(): lax.psum_scatter(query_terms, 'ctx', scatter_dimension=0, tiled=True)  79.1 us
    all_to_all x1, waiting for transfers between devices, on_device(): lax.all_to_all(jnp.stack([latent] * lax.axis_size(('head', 'query'))), ('...  29.2 us
    dot_general x4, matrix products, tile_grads(): lax.dot_general(flat_q, latent_block, (((1,), (1,)), ((), ())), preferred...  14.9 us
    all_to_all x1, starting transfers between devices, on_device(): lax.all_to_all(jnp.stack([latent] * lax.axis_size(('head', 'query'))), ('...  10.8 us
    while x40, local copies, waits for them, and re-layouts  10.2 us
    dot_general x4, matrix products, tile_grads(): lax.dot_general(dscores, flat_q, (((0,), (0,)), ((), ())), preferred_elem...  9.85 us
  transfers between devices with their start and end apart: 3, of which 3 were waited for; matrix products, arithmetic and copies ran while one was open for 3% of the time, Pallas kernels for 0%

profile of v1, /device:TPU:1, one launch (start us, length us, event | category | flops | bytes accessed | tf_op | source)
XLA Modules:
  0.0 484.0 jit_solution(8382426142184636010)
XLA Ops:
  7.2 2.5 stack.2
  9.7 10.8 %all-to-all-start = ((bf16[64,32,576]{2,1,0:T(8,128)(2,1)}), bf16[64,32,576]{2,1,0:T(8,128)(2,1)S(1)}, u32[]{:S(2)}, u32[]{:S(2)}) async-start(bf16[64,32,576]{2,1,0:T(8,128)(2,1)} %stack.2), calls=%async_computation | async-start | bytes 5242880 | tf_op jit(solution)/shard_map/all_to_all | solution.py:65
  20.5 0.0 reduce-scatter.5.cloned.1.call-start
  20.6 0.1 copy.11
  20.7 0.1 sub.60
  20.8 0.1 copy.12
  20.9 0.1 sub.59
  21.0 4.9 %copy.10 = bf16[128,16,576]{2,1,0:T(8,128)(2,1)} copy(bf16[128,16,576]{0,2,1:T(8,128)(2,1)} %param.7) | data formatting | bytes 4718592 | tf_op args[0]
  25.9 29.2 %all-to-all-done = bf16[64,32,576]{2,1,0:T(8,128)(2,1)S(1)} async-done(((bf16[64,32,576]{2,1,0:T(8,128)(2,1)}), bf16[64,32,576]{2,1,0:T(8,128)(2,1)S(1)}, u32[]{:S(2)}, u32[]{:S(2)}) %all-to-all-start) | async-done | bytes 2359328 | tf_op jit(solution)/shard_map/all_to_all | solution.py:65
  55.1 54.6 %while.16 = (s32[]{:T(128)}, f32[2048,576]{0,1:T(8,128)}, f32[4,512,576]{1,2,0:T(8,128)}, bf16[4,512,576]{2,1,0:T(8,128)(2,1)S(1)}, bf16[2048,576]{1,0:T(8,128)(...) while((s32[]{:T(128)}, f32[2048,576]{0,1:T(8,128)}, ...), condition=%wide.wide.region_1.2_spmd.clone, body=%wide.wide.region_0.1_spmd.clone.sunk | while | flops 5782700032 | bytes 94265624 | solution.py:53
  55.1 0.1 dynamic-slice_bitcast_fusion.3
  55.2 3.7 fusion.55
  58.9 1.3 fusion.56
  60.3 1.3 multiply_convert_fusion.3
  61.6 0.4 copy-done.1
  62.0 2.4 fusion.57
  64.5 2.1 select_add_fusion.3
  66.6 2.2 copy-done
  68.8 0.1 dynamic-slice_bitcast_fusion.3
  68.8 3.7 fusion.55
  72.6 1.3 fusion.56
  73.9 1.3 multiply_convert_fusion.3
  75.3 0.4 copy-done.1
  75.6 2.4 fusion.57
  78.1 2.1 select_add_fusion.3
  80.2 2.2 copy-done
  82.4 0.1 dynamic-slice_bitcast_fusion.3
  82.5 3.7 fusion.55
  86.2 1.3 fusion.56
  87.5 1.3 multiply_convert_fusion.3
  88.9 0.4 copy-done.1
  89.3 2.5 fusion.57
  91.8 2.1 select_add_fusion.3
  93.9 2.2 copy-done
  96.1 0.1 dynamic-slice_bitcast_fusion.3
  96.2 3.7 fusion.55
  99.9 1.3 fusion.56
  101.2 1.3 multiply_convert_fusion.3
  102.6 0.4 copy-done.1
  103.0 2.4 fusion.57
  105.4 2.1 select_add_fusion.3
  107.5 2.2 copy-done
  109.7 5.8 %copy.14 = f32[4,512,576]{2,1,0:T(8,128)} copy(f32[4,512,576]{1,2,0:T(8,128)} %get-tuple-element.105) | data formatting | bytes 9437184 | tf_op jit(solution)/shard_map/while | solution.py:53
  115.5 0.0 reduce-scatter.3.cloned.1.call-start
  115.5 5.4 %broadcast_multiply_fusion = f32[2048,576]{0,1:T(8,128)} fusion(f32[2048,576]{0,1:T(8,128)} %get-tuple-element.104), kind=kLoop, calls=%fused_computation.14 | loop fusion | flops 1179648 | bytes 9437184 | tf_op jit(solution)/shard_map/mul | solution.py:72
  121.0 5.8 %copy.13 = f32[2048,576]{1,0:T(8,128)} copy(f32[2048,576]{0,1:T(8,128)} %broadcast_multiply_fusion) | data formatting | bytes 9437184 | tf_op jit(solution)/shard_map/mul | solution.py:72
  126.8 271.3 %reduce-scatter.5.cloned.1.call-done = f32[32,576]{1,0:T(8,128)} async-done(((f32[2048,576]{1,0:T(8,128)}), f32[32,576]{1,0:T(8,128)}) %reduce-scatter.5.cloned.1.call-update) | async-done | bytes 73744 | tf_op jit(solution)/shard_map/reduce_scatter | solution.py:71
  398.1 79.1 %reduce-scatter.3.cloned.1.call-done = f32[64,16,576]{2,1,0:T(8,128)} async-done(((f32[128,16,576]{2,1,0:T(8,128)}), f32[64,16,576]{2,1,0:T(8,128)}) %reduce-scatter.3.cloned.1.call-update) | async-done | bytes 2359312 | tf_op jit(solution)/shard_map/reduce_scatter | solution.py:73
  (48 shorter events, 0.1 us)
Async XLA Ops:
  7.2 13.4 %copy-start.4 = (f32[128,16]{0,1:T(8,128)S(1)}, f32[128,16]{0,1:T(8,128)}, u32[]{:S(2)}) copy-start(f32[128,16]{0,1:T(8,128)} %param.10) | copy-start | bytes 24580
  7.2 13.6 %copy-start.5 = (f32[128,16]{0,1:T(8,128)S(1)}, f32[128,16]{0,1:T(8,128)}, u32[]{:S(2)}) copy-start(f32[128,16]{0,1:T(8,128)} %param.11) | copy-start | bytes 24580
  9.7 45.5 %all-to-all-start = ((bf16[64,32,576]{2,1,0:T(8,128)(2,1)}), bf16[64,32,576]{2,1,0:T(8,128)(2,1)S(1)}, u32[]{:S(2)}, u32[]{:S(2)}) async-start(bf16[64,32,576]{2,1,0:T(8,128)(2,1)} %stack.2), calls=%async_computation | async-start | bytes 5242880 | tf_op jit(solution)/shard_map/all_to_all | solution.py:65
  20.5 377.5 %reduce-scatter.5.cloned.1.call-start = ((), (), s32[]{:S(2)}) async-start(), calls=%async_computation.4 | async-start | bytes 5324800 | tf_op jit(solution)/shard_map/reduce_scatter | solution.py:71
  20.7 34.4 %copy-start.2 = (f32[128,16]{1,0:T(8,128)}, f32[128,16]{1,0:T(8,128)S(1)}, u32[]{:S(2)}) copy-start(f32[128,16]{1,0:T(8,128)S(1)} %copy.11) | copy-start | bytes 24580
  20.9 34.2 %copy-start.3 = (f32[128,16]{1,0:T(8,128)}, f32[128,16]{1,0:T(8,128)S(1)}, u32[]{:S(2)}) copy-start(f32[128,16]{1,0:T(8,128)S(1)} %copy.12) | copy-start | bytes 24580
  55.2 3.7 copy-start.6
  60.3 1.7 copy-start.1
  60.3 4.2 slice-start
  62.0 2.4 slice-start.1
  66.6 2.2 copy-start
  68.8 3.7 copy-start.6
  73.9 1.7 copy-start.1
  73.9 4.2 slice-start
  75.6 2.5 slice-start.1
  80.2 2.2 copy-start
  82.4 3.7 copy-start.6
  87.5 1.7 copy-start.1
  87.5 4.3 slice-start
  89.3 2.5 slice-start.1
  93.9 2.2 copy-start
  96.2 3.7 copy-start.6
  101.2 1.7 copy-start.1
  101.2 4.2 slice-start
  103.0 2.4 slice-start.1
  107.5 2.2 copy-start
  115.5 361.6 %reduce-scatter.3.cloned.1.call-start = ((), (), s32[]{:S(2)}) async-start(), calls=%async_computation.3 | async-start | bytes 7864320 | tf_op jit(solution)/shard_map/reduce_scatter | solution.py:73
Sparse Core Ops, SparseCore 0:
  115.6 282.4 reduce-scatter.4
  401.1 76.0 reduce-scatter.2
